TPU v7x, 128 devices: a whole 4x4x4 slice. The times are simulated.
128 devices in a mesh: col: 8 (over x, z_lo), row: 16 (over y, z_hi, core).
Axes of the slice: x: 4, y: 4, z: 4 (z_hi: 2, z_lo: 2; z = z_hi * 2 + z_lo), core: 2. Of those that a mesh axis runs over, the one named last changes fastest.
Arguments:
- covariance: float32 [12288, 12288], P('row', 'col'), may hold values from -2 to 2, as said below
- wfs_map: int32 [12288], P('row'), may hold values from 0 to 5
- noise_var: float32 [6], replicated, may hold values from 0.5 to 2
- targets: float32 [12288, 2048], P('row', 'col'), may hold values from -0.6 to 0.6
- target_pos: float32 [2, 2048], replicated, may hold values from -1 to 1
- layer_strength: float32 [35], replicated, may hold values from 0.005 to 0.05
- layer_scale: float32 [35], replicated, may hold values from 0.2 to 2
- tile_layer: int32 [16], replicated, may hold values from 0 to 34
Outputs:
- updated: float32 [12288, 12288], P('row', 'col')
- panel_factor: float32 [12288, 256], P('row')
- reconstructor: float32 [12288, 2048], P('row', 'col')
- error_cov: float32 [2048, 2048], P('row', 'col')
Inputs may be any that keep to these rules, and one draw needn't show every extreme that they name: `covariance`: symmetric and positive semidefinite; its diagonal lies between 0.5 and 2.
All inputs are finite; a program needn't handle non-finite values.
Results may differ from a plain program's by a relative error of at most 0.0003.
Values sent between devices are 32-bit elements; how exact they have to be, the bound alone decides.
No kernel may reach another device: no remote copies, remote signals or barrier semaphores. Data moves between devices by JAX's collectives and lax.ppermute only.
A program may use at most 64 MiB of HBM per device.

v0:
```python
import jax
import jax.numpy as jnp
from jax import lax
from jax.sharding import PartitionSpec as P

PB = 256
TILE = 128
precise = lax.Precision.HIGHEST


def broadcast(shard, axis, root):
    mine = lax.axis_index(axis) == root
    return lax.psum(jnp.where(mine, shard, jnp.zeros_like(shard)), axis)


def lookup(values, indices, entries):
    one_hot = (indices[:, None] == jnp.arange(entries, dtype=jnp.int32)[None, :]).astype(
        jnp.float32
    )
    return jnp.dot(one_hot, values, precision=precise)


def target_covariance(pos_rows, pos_cols, layer_rows, layer_cols, layer_strength, layer_scale):
    distance = (pos_rows[0][:, None] - pos_cols[0][None, :]) ** 2 + (
        pos_rows[1][:, None] - pos_cols[1][None, :]
    ) ** 2
    lowest = jnp.minimum(layer_rows[:, None], layer_cols[None, :])
    levels = jnp.arange(layer_strength.shape[0], dtype=jnp.int32)
    weights = layer_strength[:, None, None] / (
        1.0 + distance[None] / (layer_scale * layer_scale)[:, None, None]
    )
    return jnp.sum(jnp.where(levels[:, None, None] <= lowest[None], weights, 0.0), axis=0)


def local(
    covariance, wfs_map, noise_var, targets, target_pos, layer_strength, layer_scale, tile_layer
):
    row_count, col_count = covariance.shape
    target_width = targets.shape[1]
    row_index = lax.axis_index("row")
    col_index = lax.axis_index("col")
    row_ids = row_index * row_count + jnp.arange(row_count, dtype=jnp.int32)
    col_ids = col_index * col_count + jnp.arange(col_count, dtype=jnp.int32)
    noise_rows = lookup(noise_var, wfs_map, noise_var.shape[0])
    on_diagonal = row_ids[:, None] == col_ids[None, :]
    matrix = covariance + jnp.where(on_diagonal, noise_rows[:, None], 0.0)
    diag_block = broadcast(matrix[:PB, :PB], ("col", "row"), 0)
    factor = jnp.linalg.cholesky(diag_block)
    solved = jax.scipy.linalg.solve_triangular(factor, matrix[:, :PB].T, lower=True).T
    top_rows = jnp.concatenate([factor, jnp.zeros((row_count - PB, PB), jnp.float32)], axis=0)
    own_rows = jnp.where(row_ids[:, None] < PB, top_rows, solved)
    panel_rows = broadcast(own_rows, "col", 0)
    head_rows = jax.scipy.linalg.solve_triangular(factor, targets[:PB], lower=True)
    upper_rows = jax.scipy.linalg.solve_triangular(factor, matrix[:PB, :], lower=True)
    lead_cols = jnp.concatenate([factor.T, jnp.zeros((PB, col_count - PB), jnp.float32)], axis=1)
    upper_rows = jnp.where(col_ids[None, :] < PB, lead_cols, upper_rows)
    upper_rows, head_cols = (broadcast(upper_rows, "row", 0), broadcast(head_rows, "row", 0))
    product = jnp.dot(panel_rows, upper_rows, precision=precise)
    fill_cols = jnp.concatenate(
        [panel_rows, jnp.zeros((row_count, col_count - PB), jnp.float32)], axis=1
    )
    trailing = (row_ids[:, None] >= PB) & (col_ids[None, :] >= PB)
    updated = jnp.where(
        trailing, matrix - product, jnp.where(col_ids[None, :] < PB, fill_cols, 0.0)
    )
    head_top = jnp.concatenate(
        [head_cols, jnp.zeros((row_count - PB, target_width), jnp.float32)], axis=0
    )
    reduced = targets - jnp.dot(panel_rows, head_cols, precision=precise)
    reconstructor = jnp.where(row_ids[:, None] < PB, head_top, reduced)
    error_rows = target_width * lax.axis_size("col") // lax.axis_size("row")
    row_start = row_index * error_rows
    gathered = lax.all_gather(head_cols, "col", axis=1, tiled=True)
    head_needed = lax.dynamic_slice_in_dim(gathered, row_start, error_rows, 1)
    layer_all = jnp.repeat(tile_layer, TILE)
    col_start = col_index * target_width
    pos_rows = lax.dynamic_slice_in_dim(target_pos, row_start, error_rows, 1)
    pos_cols = lax.dynamic_slice_in_dim(target_pos, col_start, target_width, 1)
    layer_rows = lax.dynamic_slice_in_dim(layer_all, row_start, error_rows, 0)
    layer_cols = lax.dynamic_slice_in_dim(layer_all, col_start, target_width, 0)
    target_cov = target_covariance(
        pos_rows, pos_cols, layer_rows, layer_cols, layer_strength, layer_scale
    )
    error_cov = target_cov - lax.dot_general(
        head_needed,
        head_cols,
        (((0,), (0,)), ((), ())),
        precision=precise,
        preferred_element_type=jnp.float32,
    )
    return (updated, panel_rows, reconstructor, error_cov)


def solution(mesh):
    placed = (P("row", "col"), P("row"), P(), P("row", "col"), P(), P(), P(), P())
    return jax.shard_map(
        local,
        mesh=mesh,
        in_specs=placed,
        out_specs=(P("row", "col"), P("row", None), P("row", "col"), P("row", "col")),
        check_vma=False,
    )
```

profile of v0, /device:TPU:0, one launch (start us, length us, event | category | flops | bytes accessed | tf_op | source)
XLA Modules:
  0.0 518.4 jit_solution(5108484847680421361)
XLA Ops:
  7.2 0.0 all-reduce.10.cloned.1.call-start
  7.2 6.1 %copy.26 = f32[768,1536]{0,1:T(8,128)} copy(f32[768,1536]{1,0:T(8,128)} %param.8) | data formatting | bytes 9437184 | tf_op args[0]
  13.3 0.4 convolution_reduce_fusion
  13.8 2.9 select_add_fusion
  16.6 2.2 copy-done.1
  18.8 0.7 slice_select_fusion
  19.5 0.0 all-reduce.10.cloned.1.call-update
  19.6 0.0 all-reduce.14.cloned.1.call-start
  19.7 144.5 %all-reduce.10.cloned.1.call-done = f32[256,256]{0,1:T(8,128)} async-done(((f32[256,256]{0,1:T(8,128)}), f32[256,256]{0,1:T(8,128)}) %all-reduce.10.cloned.1.call-update) | async-done | bytes 262160 | tf_op jit(solution)/shard_map/psum | solution.py:13
  164.2 1.1 copy.27
  165.2 1.0 fusion.11
  166.3 11.7 %cholesky.49 = f32[128,128]{1,0:T(8,128)S(1)} custom-call(f32[128,128]{1,0:T(8,128)S(1)} %cholesky.115), custom_call_target="Cholesky" | custom-call | tf_op jit(solution)/shard_map/jit(cholesky)/cholesky | solution.py:48
  178.0 0.1 copy.28
  178.1 9.8 %custom-call.21 = f32[1,128,128]{1,2,0:T(8,128)S(1)} custom-call(f32[1,128,128]{2,1,0:T(8,128)S(1)} %get-tuple-element.43), custom_call_target="InvertDiagBlocksLowerTriangular" | custom-call | tf_op jit(solution)/shard_map/jit(cholesky)/cholesky | solution.py:48
  187.9 0.2 fusion.17
  188.1 0.1 copy.29
  188.2 0.3 convolution_subtract_fusion.5
  188.5 11.7 %cholesky.103 = f32[128,128]{1,0:T(8,128)S(1)} custom-call(f32[128,128]{1,0:T(8,128)S(1)} %convolution_subtract_fusion.5), custom_call_target="Cholesky" | custom-call | tf_op jit(solution)/shard_map/jit(cholesky)/cholesky | solution.py:48
  200.2 0.1 copy.30
  200.4 0.6 compare_reduce_fusion
  202.4 0.1 triangular_solve.72
  202.5 4.4 while.1
  202.6 0.6 fusion.47
  203.2 1.4 dynamic-slice.11
  204.6 0.1 copy.45
  204.7 0.6 fusion.47
  205.3 1.4 dynamic-slice.11
  206.7 0.1 copy.45
  206.8 19.7 %custom-call.22 = f32[2,128,128]{1,2,0:T(8,128)S(1)} custom-call(f32[2,128,128]{2,1,0:T(8,128)S(1)} %get-tuple-element.11), custom_call_target="InvertDiagBlocksLowerTriangular" | custom-call | tf_op jit(solution)/shard_map/jit(_solve_triangular)/triangular_solve | solution.py:49
  226.5 2.0 fusion.5
  228.5 1.2 fusion.15
  229.8 1.2 convolution_subtract_fusion.4
  231.0 0.1 copy.33
  231.1 2.5 convolution_subtract_fusion
  233.6 0.9 fusion.21
  234.5 0.4 fusion.20
  234.9 0.7 maximum_select_fusion.1
  235.6 1.3 fusion.3
  237.0 0.0 all-reduce.14.cloned.1.call-update
  237.0 0.0 all-reduce.12.cloned.1.call-start
  237.1 1.2 slice_bitcast_fusion
  238.3 0.5 fusion.9
  238.9 0.5 convolution_subtract_fusion.2
  239.4 0.5 fusion.22
  239.9 1.0 fusion.8
  240.9 0.0 all-gather.2.cloned.1.call-start
  240.9 137.2 %all-reduce.14.cloned.1.call-done = (f32[256,1536]{1,0:T(8,128)}, f32[256,256]{0,1:T(8,128)}) async-done(((f32[256,1536]{1,0:T(8,128)}, f32[256,256]{0,1:T(8,128)}), (f32[256,1536]{1,0:T(8,128)}, f32[256,256]{0,1:T(8,128)})) %all-reduce.14.cloned.1.call-update) | async-done | bytes 1835024 | tf_op jit(solution)/shard_map/psum | solution.py:13
  378.1 0.3 copy.35
  378.5 0.1 broadcast_bitcast_fusion
  378.5 0.1 dynamic_slice.16
  378.6 0.1 dynamic_slice.15
  378.7 0.7 constant_dynamic-slice_fusion.2
  379.4 0.8 constant_dynamic-slice_fusion.1
  380.2 0.1 broadcast_minimum_fusion
  380.3 0.1 multiply_add_fusion
  380.4 1.2 fusion.2
  381.6 76.2 %all-reduce.12.cloned.1.call-done = f32[768,256]{0,1:T(8,128)} async-done(((f32[768,256]{0,1:T(8,128)}), f32[768,256]{0,1:T(8,128)}) %all-reduce.12.cloned.1.call-update) | async-done | bytes 786448 | tf_op jit(solution)/shard_map/psum | solution.py:13
  457.8 2.3 copy.38
  460.1 9.2 %select_select_fusion = f32[768,1536]{0,1:T(8,128)} fusion(f32[768,256]{0,1:T(8,128)} %all-reduce.12.cloned.1.call-done, f32[768,1536]{0,1:T(8,128)} %copy-done.1, f32[256,1536]{1,0:T(8,128)S(1)} %copy-done.4, pred[1536]{0:T(1024)(128)(4,1)S(1)} %fusion.26, pred[768]{0:T(1024)(128)(4,1)S(1)} %fusion.29, pred[1536]{0:T(1024)(128)(4,1)S(1)} %fusion.27), kind=kOutput, calls=%fused_computation.2 | convolution fusion | flops 3628597248 | bytes 11800320 | tf_op jit(solution)/shard_map/dot_general | solution.py:58
  469.3 6.1 %copy.37 = f32[768,1536]{1,0:T(8,128)} copy(f32[768,1536]{0,1:T(8,128)} %select_select_fusion) | data formatting | bytes 9437184
  475.4 0.9 fusion.4
  476.3 1.1 copy.39
  477.5 32.4 %all-gather.2.cloned.1.call-done = f32[256,2048]{0,1:T(8,128)} async-done(((f32[256,256]{0,1:T(8,128)}), f32[256,2048]{0,1:T(8,128)}) %all-gather.2.cloned.1.call-update) | async-done | bytes 2097168 | tf_op jit(solution)/shard_map/all_gather | solution.py:73
  509.9 2.0 convolution_subtract_fusion.3
  (42 shorter events, 0.3 us)
Async XLA Ops:
  7.2 371.3 %copy-start = (s32[16]{0:T(128)S(1)}, s32[16]{0:T(128)}, u32[]{:S(2)}) copy-start(s32[16]{0:T(128)} %param.15) | copy-start | bytes 196
  7.2 157.0 %all-reduce.10.cloned.1.call-start = ((), (), s32[]{:S(2)}) async-start(), calls=%async_computation | async-start | bytes 524288 | tf_op jit(solution)/shard_map/psum | solution.py:13
  7.2 6.1 %copy-start.7 = (s32[768]{0:T(1024)S(1)}, s32[768]{0:T(1024)}, u32[]{:S(2)}) copy-start(s32[768]{0:T(1024)} %param.9) | copy-start | bytes 9220
  7.2 6.1 %copy-start.8 = (f32[6]{0:T(128)S(1)}, f32[6]{0:T(128)}, u32[]{:S(2)}) copy-start(f32[6]{0:T(128)} %param.10) | copy-start | bytes 76
  16.6 2.2 copy-start.1
  19.6 358.5 %all-reduce.14.cloned.1.call-start = ((), (), s32[]{:S(2)}) async-start(), calls=%async_computation.3 | async-start | bytes 3670016 | tf_op jit(solution)/shard_map/psum | solution.py:13
  237.0 141.2 %copy-start.5 = (f32[768,256]{1,0:T(8,128)S(1)}, f32[768,256]{1,0:T(8,128)}, u32[]{:S(2)}) copy-start(f32[768,256]{1,0:T(8,128)} %param.11) | copy-start | bytes 2359300
  237.0 141.4 %copy-start.9 = (f32[35]{0:T(128)S(1)}, f32[35]{0:T(128)}, u32[]{:S(2)}) copy-start(f32[35]{0:T(128)} %param.14) | copy-start | bytes 424
  237.0 220.8 %all-reduce.12.cloned.1.call-start = ((), (), s32[]{:S(2)}) async-start(), calls=%async_computation.1 | async-start | bytes 1572864 | tf_op jit(solution)/shard_map/psum | solution.py:13
  237.1 143.3 %copy-start.6 = (f32[35]{0:T(128)S(1)}, f32[35]{0:T(128)}, u32[]{:S(2)}) copy-start(f32[35]{0:T(128)} %param.13) | copy-start | bytes 424
  240.9 269.0 %all-gather.2.cloned.1.call-start = ((), (), s32[]{:S(2)}) async-start(), calls=%async_computation.2 | async-start | bytes 2359296 | tf_op jit(solution)/shard_map/all_gather | solution.py:73
  378.1 82.0 %copy-start.4 = (f32[256,1536]{1,0:T(8,128)S(1)}, f32[256,1536]{1,0:T(8,128)}, u32[]{:S(2)}) copy-start(f32[256,1536]{1,0:T(8,128)} %get-tuple-element.36) | copy-start | bytes 4718596
  469.3 6.1 %copy-start.2 = (f32[768,256]{0,1:T(8,128)S(1)}, f32[768,256]{0,1:T(8,128)}, u32[]{:S(2)}) copy-start(f32[768,256]{0,1:T(8,128)} %all-reduce.12.cloned.1.call-done) | copy-start | bytes 2359300
  469.3 6.1 %copy-start.3 = (f32[256,256]{0,1:T(8,128)S(1)}, f32[256,256]{0,1:T(8,128)}, u32[]{:S(2)}) copy-start(f32[256,256]{0,1:T(8,128)} %get-tuple-element.37) | copy-start | bytes 786436
Sparse Core Ops, SparseCore 0:
  19.7 144.4 all-reduce.9
  237.1 140.9 all-reduce.13
  381.3 76.4 all-reduce.11
  459.3 50.5 all-gather.1
where the time goes:
time: 519 us; the launch traced here: 518 us
  waiting for transfers between devices  390 us (75%)
  other arithmetic  62.7 us (12%)
  local copies, waits for them, and re-layouts  26.8 us (5%)
  matrix products  22.7 us (4%)
  between operations  15.5 us (3%)
    psum x3, waiting for transfers between devices, broadcast(): return lax.psum(jnp.where(mine, shard, jnp.zeros_like(shard)), axis)  358 us
    another operation x6, other arithmetic, local(): factor = jnp.linalg.cholesky(diag_block)  33.9 us
    all_gather x1, waiting for transfers between devices, local(): gathered = lax.all_gather(head_cols, 'col', axis=1, tiled=True)  32.4 us
    another operation x3, other arithmetic, local(): jax.scipy.linalg.solve_triangular(factor, matrix[:, :PB].T, lower=True)  19.7 us
    unnamed x25, local copies, waits for them, and re-layouts  18.1 us
  transfers between devices with their start and end apart: 4, of which 4 were waited for; matrix products, arithmetic and copies ran while one was open for 5% of the time, Pallas kernels for 0%

commit v1 on v0

--- a/solution.py
+++ b/solution.py
@@ -70,7 +70,9 @@
     reconstructor = jnp.where(row_ids[:, None] < PB, head_top, reduced)
     error_rows = target_width * lax.axis_size("col") // lax.axis_size("row")
     row_start = row_index * error_rows
-    gathered = lax.all_gather(head_cols, "col", axis=1, tiled=True)
+    gathered = jnp.concatenate(
+        lax.all_to_all(jnp.stack([head_cols] * lax.axis_size("col")), "col", 0, 0), axis=1
+    )
     head_needed = lax.dynamic_slice_in_dim(gathered, row_start, error_rows, 1)
     layer_all = jnp.repeat(tile_layer, TILE)
     col_start = col_index * target_width

time: 519 us -> 499 us (0.961)
  waiting for transfers between devices: 390 us -> 365 us
    all_gather x1 -> x0, waiting for transfers between devices: 32.4 us -> none  [local(): gathered = lax.all_gather(head_cols, 'col', axis=1, tiled=True)]
    psum x3, waiting for transfers between devices: 358 us -> 365 us  [broadcast(): return lax.psum(jnp.where(mine, shard, jnp.zeros_like(shard)), axis)]
  transfers between devices with their start and end apart: 4 -> 4, of which waited for: 4 -> 3; matrix products, arithmetic and copies ran while one was open for 5% -> 6% of each run, Pallas kernels for 0% -> 0%
where the time goes in v1:
time: 499 us; the launch traced here: 498 us
  waiting for transfers between devices  365 us (73%)
  other arithmetic  62.7 us (13%)
  local copies, waits for them, and re-layouts  29.4 us (6%)
  matrix products  20.9 us (4%)
  between operations  15.4 us (3%)
    psum x3, waiting for transfers between devices, broadcast(): return lax.psum(jnp.where(mine, shard, jnp.zeros_like(shard)), axis)  365 us
    another operation x6, other arithmetic, local(): factor = jnp.linalg.cholesky(diag_block)  33.9 us
    another operation x3, other arithmetic, local(): jax.scipy.linalg.solve_triangular(factor, matrix[:, :PB].T, lower=True)  19.7 us
    unnamed x25, local copies, waits for them, and re-layouts  18.1 us
  transfers between devices with their start and end apart: 4, of which 3 were waited for; matrix products, arithmetic and copies ran while one was open for 6% of the time, Pallas kernels for 0%

profile of v1, /device:TPU:0, one launch (start us, length us, event | category | flops | bytes accessed | tf_op | source)
XLA Modules:
  0.0 498.2 jit_solution(16146570833556749602)
XLA Ops:
  7.2 0.0 all-reduce.10.cloned.1.call-start
  7.2 6.1 %copy.41 = f32[768,1536]{0,1:T(8,128)} copy(f32[768,1536]{1,0:T(8,128)} %param.8) | data formatting | bytes 9437184 | tf_op args[0]
  13.3 0.4 convolution_reduce_fusion
  13.8 2.9 select_add_fusion
  16.6 2.2 copy-done.1
  18.8 0.7 slice_select_fusion
  19.5 0.0 all-reduce.10.cloned.1.call-update
  19.6 0.0 all-reduce.14.cloned.1.call-start
  19.6 0.7 constant_dynamic-slice_fusion.2
  20.3 0.1 broadcast_bitcast_fusion
  20.4 143.7 %all-reduce.10.cloned.1.call-done = f32[256,256]{0,1:T(8,128)} async-done(((f32[256,256]{0,1:T(8,128)}), f32[256,256]{0,1:T(8,128)}) %all-reduce.10.cloned.1.call-update) | async-done | bytes 262160 | tf_op jit(solution)/shard_map/psum | solution.py:13
  164.2 1.1 copy.42
  165.2 1.0 fusion.11
  166.3 11.7 %cholesky.49 = f32[128,128]{1,0:T(8,128)S(1)} custom-call(f32[128,128]{1,0:T(8,128)S(1)} %cholesky.115), custom_call_target="Cholesky" | custom-call | tf_op jit(solution)/shard_map/jit(cholesky)/cholesky | solution.py:48
  178.0 0.1 copy.43
  178.1 9.8 %custom-call.21 = f32[1,128,128]{1,2,0:T(8,128)S(1)} custom-call(f32[1,128,128]{2,1,0:T(8,128)S(1)} %get-tuple-element.51), custom_call_target="InvertDiagBlocksLowerTriangular" | custom-call | tf_op jit(solution)/shard_map/jit(cholesky)/cholesky | solution.py:48
  187.9 0.2 fusion.17
  188.1 0.1 copy.44
  188.2 0.3 convolution_subtract_fusion.5
  188.5 11.7 %cholesky.103 = f32[128,128]{1,0:T(8,128)S(1)} custom-call(f32[128,128]{1,0:T(8,128)S(1)} %convolution_subtract_fusion.5), custom_call_target="Cholesky" | custom-call | tf_op jit(solution)/shard_map/jit(cholesky)/cholesky | solution.py:48
  200.2 0.1 copy.45
  200.4 0.6 compare_reduce_fusion
  202.4 0.1 triangular_solve.72
  202.5 4.4 while.1
  202.6 0.6 fusion.47
  203.2 1.4 dynamic-slice.11
  204.6 0.1 copy.62
  204.7 0.6 fusion.47
  205.3 1.4 dynamic-slice.11
  206.7 0.1 copy.62
  206.8 19.7 %custom-call.22 = f32[2,128,128]{1,2,0:T(8,128)S(1)} custom-call(f32[2,128,128]{2,1,0:T(8,128)S(1)} %get-tuple-element.11), custom_call_target="InvertDiagBlocksLowerTriangular" | custom-call | tf_op jit(solution)/shard_map/jit(_solve_triangular)/triangular_solve | solution.py:49
  226.5 2.0 fusion.5
  228.5 0.3 fusion.15
  228.8 0.3 convolution_subtract_fusion.4
  229.2 0.1 copy.49
  229.3 2.5 convolution_subtract_fusion
  231.8 0.9 fusion.21
  232.7 0.4 fusion.20
  233.1 0.7 maximum_select_fusion.1
  233.8 1.3 fusion.3
  235.2 0.0 all-reduce.14.cloned.1.call-update
  235.2 0.0 all-reduce.12.cloned.1.call-start
  235.3 0.3 copy.51
  235.6 0.1 dynamic_slice.15
  235.6 0.1 dynamic_slice.16
  235.7 0.8 constant_dynamic-slice_fusion.1
  236.5 0.1 broadcast_minimum_fusion
  236.6 0.1 multiply_add_fusion
  236.7 1.2 slice_bitcast_fusion
  237.9 0.5 fusion.9
  238.5 0.5 convolution_subtract_fusion.2
  239.0 0.5 fusion.22
  239.5 1.0 fusion.8
  240.5 135.7 %all-reduce.14.cloned.1.call-done = (f32[256,1536]{1,0:T(8,128)}, f32[256,256]{0,1:T(8,128)}) async-done(((f32[256,1536]{1,0:T(8,128)}, f32[256,256]{0,1:T(8,128)}), (f32[256,1536]{1,0:T(8,128)}, f32[256,256]{0,1:T(8,128)})) %all-reduce.14.cloned.1.call-update) | async-done | bytes 1835024 | tf_op jit(solution)/shard_map/psum | solution.py:13
  376.2 2.6 stack.2
  378.9 4.6 all-to-all-start
  383.5 1.2 fusion.2
  384.7 85.4 %all-reduce.12.cloned.1.call-done = f32[768,256]{0,1:T(8,128)} async-done(((f32[768,256]{0,1:T(8,128)}), f32[768,256]{0,1:T(8,128)}) %all-reduce.12.cloned.1.call-update) | async-done | bytes 786448 | tf_op jit(solution)/shard_map/psum | solution.py:13
  470.0 2.3 copy.54
  472.3 9.2 %select_select_fusion = f32[768,1536]{0,1:T(8,128)} fusion(f32[768,256]{0,1:T(8,128)} %all-reduce.12.cloned.1.call-done, f32[768,1536]{0,1:T(8,128)} %copy-done.1, f32[256,1536]{1,0:T(8,128)S(1)} %copy-done.4, pred[1536]{0:T(1024)(128)(4,1)S(1)} %fusion.26, pred[768]{0:T(1024)(128)(4,1)S(1)} %fusion.29, pred[1536]{0:T(1024)(128)(4,1)S(1)} %fusion.27), kind=kOutput, calls=%fused_computation.2 | convolution fusion | flops 3628597248 | bytes 11800320 | tf_op jit(solution)/shard_map/dot_general | solution.py:58
  481.5 6.1 %copy.53 = f32[768,1536]{1,0:T(8,128)} copy(f32[768,1536]{0,1:T(8,128)} %select_select_fusion) | data formatting | bytes 9437184
  487.6 0.9 fusion.4
  488.5 1.1 copy.55
  489.7 2.0 convolution_subtract_fusion.3
  (42 shorter events, 0.3 us)
Async XLA Ops:
  7.2 13.2 %copy-start = (s32[16]{0:T(128)S(1)}, s32[16]{0:T(128)}, u32[]{:S(2)}) copy-start(s32[16]{0:T(128)} %param.15) | copy-start | bytes 196
  7.2 157.0 %all-reduce.10.cloned.1.call-start = ((), (), s32[]{:S(2)}) async-start(), calls=%async_computation.1 | async-start | bytes 524288 | tf_op jit(solution)/shard_map/psum | solution.py:13
  7.2 6.1 %copy-start.7 = (s32[768]{0:T(1024)S(1)}, s32[768]{0:T(1024)}, u32[]{:S(2)}) copy-start(s32[768]{0:T(1024)} %param.9) | copy-start | bytes 9220
  7.2 6.1 %copy-start.8 = (f32[6]{0:T(128)S(1)}, f32[6]{0:T(128)}, u32[]{:S(2)}) copy-start(f32[6]{0:T(128)} %param.10) | copy-start | bytes 76
  16.6 2.2 copy-start.1
  18.8 209.7 %copy-start.5 = (f32[768,256]{1,0:T(8,128)S(1)}, f32[768,256]{1,0:T(8,128)}, u32[]{:S(2)}) copy-start(f32[768,256]{1,0:T(8,128)} %param.11) | copy-start | bytes 2359300
  19.6 356.7 %all-reduce.14.cloned.1.call-start = ((), (), s32[]{:S(2)}) async-start(), calls=%async_computation.3 | async-start | bytes 3670016 | tf_op jit(solution)/shard_map/psum | solution.py:13
  231.8 3.7 copy-start.9
  235.2 234.8 %all-reduce.12.cloned.1.call-start = ((), (), s32[]{:S(2)}) async-start(), calls=%async_computation.2 | async-start | bytes 1572864 | tf_op jit(solution)/shard_map/psum | solution.py:13
  239.5 143.9 %copy-start.6 = (f32[35]{0:T(128)S(1)}, f32[35]{0:T(128)}, u32[]{:S(2)}) copy-start(f32[35]{0:T(128)} %param.13) | copy-start | bytes 424
  376.2 96.1 %copy-start.4 = (f32[256,1536]{1,0:T(8,128)S(1)}, f32[256,1536]{1,0:T(8,128)}, u32[]{:S(2)}) copy-start(f32[256,1536]{1,0:T(8,128)} %get-tuple-element.44) | copy-start | bytes 4718596
  378.9 110.8 %all-to-all-start = ((f32[8,256,256]{1,2,0:T(8,128)}), f32[8,256,256]{1,2,0:T(8,128)}, u32[]{:S(2)}, u32[]{:S(2)}) async-start(f32[8,256,256]{1,2,0:T(8,128)} %stack.2), calls=%async_computation | async-start | bytes 4194304 | tf_op jit(solution)/shard_map/all_to_all | solution.py:74
  481.5 6.1 %copy-start.2 = (f32[768,256]{0,1:T(8,128)S(1)}, f32[768,256]{0,1:T(8,128)}, u32[]{:S(2)}) copy-start(f32[768,256]{0,1:T(8,128)} %all-reduce.12.cloned.1.call-done) | copy-start | bytes 2359300
  481.5 6.1 %copy-start.3 = (f32[256,256]{0,1:T(8,128)S(1)}, f32[256,256]{0,1:T(8,128)}, u32[]{:S(2)}) copy-start(f32[256,256]{0,1:T(8,128)} %get-tuple-element.45) | copy-start | bytes 786436
Sparse Core Ops, SparseCore 0:
  19.7 144.4 all-reduce.9
  235.3 140.8 all-reduce.13
  379.5 90.5 all-reduce.11
